TPU v7x, 256 devices: a whole 4x4x8 slice. The times are simulated.
256 devices in a mesh: expert: 8 (over x, core), context: 32 (over y, z).
Axes of the slice: x: 4, y: 4, z: 8, core: 2. Of those that a mesh axis runs over, the one named last changes fastest.
Arguments:
- hidden: bfloat16 [8, 4096, 2048], P('expert', 'context'), may hold values from -6 to 6
- query: bfloat16 [8, 4096, 2048], P('expert', 'context'), may hold values from -120 to 120
- keys: bfloat16 [8, 4096, 512], P('expert', 'context'), may hold values from -6 to 6
- values: bfloat16 [8, 4096, 512], P('expert', 'context'), may hold values from -6 to 6
- x_inner: bfloat16 [8, 4096, 4096], P('expert', 'context'), may hold values from -6 to 6
- z_gate: bfloat16 [8, 4096, 4096], P('expert', 'context'), may hold values from -6 to 6
- dt_raw: bfloat16 [8, 4096, 4096], P('expert', 'context'), may hold values from -5 to 5
- b_proj: float32 [8, 4096, 16], P('expert', 'context'), may hold values from -0.6 to 0.6
- c_proj: float32 [8, 4096, 16], P('expert', 'context'), may hold values from -0.6 to 0.6
- conv_weight: float32 [4, 4096], replicated, may hold values from -3 to 3
- conv_bias: float32 [4096], replicated, may hold values from -3 to 3
- dt_bias: float32 [4096], replicated, may hold values from -0.5 to 0.5
- a_rate: float32 [16, 4096], replicated, may hold values from 7.324219e-05 to 0.05
- skip_gain: float32 [4096], replicated, may hold values from 0.5 to 1.5
- mamba_vector: float32 [4096], replicated, may hold values from -0.09375 to 0.09375
- attn_vector: float32 [2048], replicated, may hold values from -0.125 to 0.125
- impact_vector: float32 [2048], replicated, may hold values from -0.125 to 0.125
- norm_gain: float32 [2048], replicated, may hold values from 0.5 to 1.5
- expert_gate: bfloat16 [16, 2048, 7168], P('expert', None, 'context'), may hold values from -0.125 to 0.125
- expert_up: bfloat16 [16, 2048, 7168], P('expert', None, 'context'), may hold values from -0.125 to 0.125
- expert_vector: float32 [16, 7168], P('expert', 'context'), may hold values from -0.0625 to 0.0625
- routes: int32 [8, 4096, 2], P('expert', 'context'), may hold values from 0 to 15, all different within a row
- route_gate: float32 [8, 4096, 2], P('expert', 'context'), may hold values from 0.1 to 0.9
- lengths: int32 [8], replicated, may hold values from 1 to 4096, 20480 in all
- term_ids: int32 [8, 4096], P('expert', 'context'), may hold values from 0 to 65535
Outputs:
- token_impacts: float32 [8, 4096], P('expert', 'context')
- term_impacts: float32 [8, 65536], P('expert', 'context')
All inputs are finite; a program needn't handle non-finite values.
Results may differ from a plain program's by a relative error of at most 0.009.
Values may be sent and summed in bfloat16 or wider, within the bound.
A program may use at most 192 MiB of HBM per device.

v0:
```python
import jax
import jax.numpy as jnp
from jax import lax
from jax.sharding import PartitionSpec as P

H = 16
HD = 128
KVH = 4
KCONV = 4
VOCAB = 65536
big_negative = -1e30
norm_eps = 1e-06


def passed_along(x, axis, by):
    devices = lax.axis_size(axis)
    pairs = [(i, i + by) for i in range(devices) if 0 <= i + by < devices]
    return lax.ppermute(x, axis, pairs)


def prefix(x, axis, join, neutral):
    place = lax.axis_index(axis)
    gathered = jax.tree.map(
        lambda a, kind: lax.all_gather(a.astype(kind), axis), x, (jnp.bfloat16, jnp.bfloat16)
    )
    state = jax.tree.map(lambda a, e: jnp.zeros_like(a) + jnp.asarray(e, a.dtype), x, neutral)

    def one(turn, state):
        return join(
            state,
            jax.tree.map(
                lambda a, own: lax.dynamic_index_in_dim(a, turn, 0, False).astype(own.dtype),
                gathered,
                x,
            ),
        )

    return lax.fori_loop(0, place, one, state)


def shards(
    hidden,
    query,
    keys,
    values,
    x_inner,
    z_gate,
    dt_raw,
    b_proj,
    c_proj,
    conv_weight,
    conv_bias,
    dt_bias,
    a_rate,
    skip_gain,
    mamba_vector,
    attn_vector,
    impact_vector,
    norm_gain,
    expert_gate,
    expert_up,
    expert_vector,
    routes,
    route_gate,
    lengths,
    term_ids,
):
    tokens_here = hidden.shape[1]
    doc_index = lax.axis_index("expert")
    shard_index = lax.axis_index("context")
    doc_length = lax.dynamic_index_in_dim(lengths, doc_index, 0, False)
    positions = shard_index * tokens_here + jnp.arange(tokens_here, dtype=jnp.int32)
    live_rows = positions < doc_length
    groups = H // KVH
    score_scale = HD ** (-0.5)
    queries = query[0].reshape(tokens_here, KVH, groups, HD)

    def key_block(carried, kv_block, first_key):
        running_max, running_sum, running_out = carried
        key_rows, value_rows = kv_block
        block_width = key_rows.shape[0]
        key_heads = key_rows.reshape(block_width, KVH, HD)
        value_heads = value_rows.reshape(block_width, KVH, HD)
        scores = (
            jnp.einsum("tgqd,rgd->gqtr", queries, key_heads, preferred_element_type=jnp.float32)
            * score_scale
        )
        key_positions = first_key + jnp.arange(block_width, dtype=jnp.int32)
        allowed = key_positions[None, :] <= positions[:, None]
        scores = jnp.where(allowed, scores, big_negative)
        new_max = jnp.maximum(running_max, jnp.max(scores, axis=-1))
        exp_scores = jnp.where(allowed, jnp.exp(scores - new_max[..., None]), 0.0)
        factor = jnp.exp(running_max - new_max)
        running_sum = running_sum * factor + jnp.sum(exp_scores, axis=-1)
        running_out = running_out * factor[..., None] + jnp.einsum(
            "gqtr,rgd->gqtd",
            exp_scores.astype(jnp.bfloat16),
            value_heads,
            preferred_element_type=jnp.float32,
        )
        return (new_max, running_sum, running_out)

    start_state = (
        jnp.full((KVH, groups, tokens_here), big_negative, jnp.float32),
        jnp.zeros((KVH, groups, tokens_here), jnp.float32),
        jnp.zeros((KVH, groups, tokens_here, HD), jnp.float32),
    )
    key_piece = lax.all_gather(keys[0], "context", axis=0, tiled=True)
    value_piece = lax.all_gather(values[0], "context", axis=0, tiled=True)
    piece_rows = key_piece.shape[0]
    block_rows = 512

    def one_block(inner_state, offset):
        kv_block = (
            lax.dynamic_slice_in_dim(key_piece, offset, block_rows, 0),
            lax.dynamic_slice_in_dim(value_piece, offset, block_rows, 0),
        )
        updated = key_block(inner_state, kv_block, offset)
        return (updated, None)

    offsets = jnp.arange(0, piece_rows, block_rows, dtype=jnp.int32)
    final_state = lax.scan(one_block, start_state, offsets)[0]
    running_sum = final_state[1]
    attended = final_state[2] / jnp.where(running_sum > 0.0, running_sum, 1.0)[..., None]
    attended = (
        jnp.transpose(attended, (2, 0, 1, 3)).reshape(tokens_here, H * HD).astype(jnp.bfloat16)
    )
    attn_score = jnp.sum(attended.astype(jnp.float32) * attn_vector[None, :], axis=-1)
    inner_rows = x_inner[0]
    conv_rim = passed_along(inner_rows[tokens_here - (KCONV - 1) :], "context", 1)
    extended = jnp.concatenate([conv_rim, inner_rows], axis=0).astype(jnp.float32)
    conv_sum = conv_bias[None, :]
    for tap_index in range(KCONV):
        conv_sum = (
            conv_sum
            + conv_weight[tap_index][None, :] * extended[tap_index : tap_index + tokens_here]
        )
    conved = jax.nn.silu(conv_sum)
    step_size = jax.nn.softplus(dt_raw[0].astype(jnp.float32) + dt_bias[None, :])
    neg_rate = -a_rate
    b_rows = b_proj[0]
    c_rows = c_proj[0]

    def emit_rows(carried, per_step):
        size_now, b_now, c_now, x_now = per_step
        carried = (
            jnp.exp(size_now[None, :] * neg_rate) * carried
            + (size_now * x_now)[None, :] * b_now[:, None]
        )
        return (carried, jnp.sum(c_now[:, None] * carried, axis=0))

    zero_state = jnp.zeros(a_rate.shape, jnp.float32)
    local_end, local_outputs = lax.scan(emit_rows, zero_state, (step_size, b_rows, c_rows, conved))
    cumulative = jnp.cumsum(step_size, axis=0)
    through = jnp.exp(neg_rate * cumulative[tokens_here - 1][None, :])

    def chain(earlier_part, later_part):
        return (earlier_part[0] * later_part[0], later_part[0] * earlier_part[1] + later_part[1])

    chain_out = prefix((through, local_end), "context", chain, (jnp.ones_like(through), zero_state))
    incoming = chain_out[1]
    row_group = 32
    group_count = tokens_here // row_group

    def carried_in(operands):
        cumulative_rows, c_group = operands
        decayed = jnp.exp(cumulative_rows[:, None, :] * neg_rate[None, :, :])
        return jnp.sum(c_group[:, :, None] * decayed * incoming[None, :, :], axis=1)

    correction = lax.map(
        carried_in,
        (
            cumulative.reshape(group_count, row_group, cumulative.shape[1]),
            c_rows.reshape(group_count, row_group, c_rows.shape[1]),
        ),
    )
    outputs = local_outputs + correction.reshape(tokens_here, cumulative.shape[1])
    mamba_out = (
        (outputs + skip_gain[None, :] * conved) * jax.nn.silu(z_gate[0].astype(jnp.float32))
    ).astype(jnp.bfloat16)
    mamba_score = jnp.sum(mamba_out.astype(jnp.float32) * mamba_vector[None, :], axis=-1)
    hidden_rows = hidden[0].astype(jnp.float32)
    mean_square = jnp.mean(hidden_rows * hidden_rows, axis=-1, keepdims=True)
    normed = (hidden_rows * lax.rsqrt(mean_square + norm_eps) * norm_gain[None, :]).astype(
        jnp.bfloat16
    )
    axis_experts = lax.axis_size("expert")
    local_experts = expert_gate.shape[0]
    all_experts = axis_experts * local_experts
    capacity = tokens_here * 5 // 64
    expert_ids = jnp.arange(all_experts, dtype=jnp.int32)
    route_rows = routes[0]
    matches = (route_rows[:, :, None] == expert_ids[None, None, :]).astype(jnp.int32)
    chosen = jnp.sum(matches, axis=1) * live_rows[:, None].astype(jnp.int32)
    before = jnp.cumsum(chosen, axis=0) - chosen
    slot_ids = jnp.arange(capacity, dtype=jnp.int32)
    placed = (chosen[:, :, None] == 1) & (before[:, :, None] == slot_ids[None, None, :])
    placed = placed.reshape(tokens_here, axis_experts, local_experts, capacity)
    outgoing = jnp.einsum(
        "tilc,td->licd", placed.astype(jnp.bfloat16), normed, preferred_element_type=jnp.float32
    ).astype(jnp.bfloat16)
    arrived = lax.all_to_all(outgoing, "expert", split_axis=1, concat_axis=1, tiled=True)
    slot_rows = arrived.reshape(local_experts, axis_experts * capacity, normed.shape[1])
    row_piece = lax.all_gather(slot_rows, "context", axis=1, tiled=True)
    gate_part = jnp.einsum(
        "lrd,ldf->lrf", row_piece, expert_gate, preferred_element_type=jnp.float32
    )
    up_part = jnp.einsum("lrd,ldf->lrf", row_piece, expert_up, preferred_element_type=jnp.float32)
    inner_units = (jax.nn.silu(gate_part) * up_part).astype(jnp.bfloat16)
    partial_terms = jnp.sum(inner_units.astype(jnp.float32) * expert_vector[:, None, :], axis=-1)
    slot_values = lax.psum_scatter(partial_terms, "context", scatter_dimension=1, tiled=True)
    returned = lax.all_to_all(
        slot_values.reshape(local_experts, axis_experts, capacity),
        "expert",
        split_axis=1,
        concat_axis=1,
        tiled=True,
    )
    per_expert = jnp.einsum(
        "tilc,lic->til", placed.astype(jnp.float32), returned, precision=lax.Precision.HIGHEST
    ).reshape(tokens_here, all_experts)
    gate_weights = jnp.sum(route_gate[0][:, :, None] * matches.astype(jnp.float32), axis=1)
    expert_score = jnp.sum(per_expert * gate_weights, axis=-1)
    base_score = jnp.sum(hidden_rows * impact_vector[None, :], axis=-1)
    score = base_score + attn_score + mamba_score + expert_score
    impacts = jnp.where(live_rows, jax.nn.relu(score), 0.0)
    shard_count = lax.axis_size("context")
    vocab_block = VOCAB // shard_count
    pooled = jnp.zeros((VOCAB,), jnp.float32).at[term_ids[0]].max(impacts)
    everything = lax.pmax(pooled.astype(jnp.bfloat16), "context").astype(pooled.dtype)
    own_block = lax.dynamic_slice_in_dim(everything, shard_index * vocab_block, vocab_block, 0)
    return (impacts[None, :], own_block[None, :])


def solution(mesh):
    placed = (
        P("expert", "context", None),
        P("expert", "context", None),
        P("expert", "context", None),
        P("expert", "context", None),
        P("expert", "context", None),
        P("expert", "context", None),
        P("expert", "context", None),
        P("expert", "context", None),
        P("expert", "context", None),
        P(),
        P(),
        P(),
        P(),
        P(),
        P(),
        P(),
        P(),
        P(),
        P("expert", None, "context"),
        P("expert", None, "context"),
        P("expert", "context"),
        P("expert", "context", None),
        P("expert", "context", None),
        P(),
        P("expert", "context"),
    )
    return jax.shard_map(
        shards,
        mesh=mesh,
        in_specs=placed,
        out_specs=(P("expert", "context"), P("expert", "context")),
        check_vma=False,
    )
```

profile of v0, /device:TPU:2, one launch (start us, length us, event | category | flops | bytes accessed | tf_op | source)
XLA Modules:
  0.0 1122.7 jit_solution(12694423566203048189)
XLA Ops:
  12.3 3.8 collective-permute-start
  16.1 3.8 compare_select_fusion
  19.9 4.7 reduce_window_sum.22
  31.9 441.6 %while.57 = (s32[]{:T(128)}, f32[16,4096]{1,0:T(8,128)S(1)}, f32[128,4096]{1,0:T(8,128)}, f32[128,4096]{1,0:T(8,128)}, f32[16,4096]{1,0:T(8,128)S(1)}, /*index=5...) while((s32[]{:T(128)}, f32[16,4096]{1,0:T(8,128)S(1)}, ...), condition=%wide.region_8.9_spmd.clone.clone, body=%wide.region_6.8_spmd.clone.sunk.clone | while | flops 458755 | bytes 934379 | solution.py:153
  481.0 15.0 %all_to_all.10 = bf16[2,8,10,2048]{3,0,2,1:T(2,128)(2,1)S(1)} all-to-all(bf16[2,8,10,2048]{3,0,2,1:T(2,128)(2,1)S(1)} %copy.85), channel_id=1, replica_groups=mesh['expert'=8,'context'=32] {'expert'}, dimensions={1} | all-to-all | bytes 1310720 | tf_op jit(solution)/shard_map/all_to_all | solution.py:202
  498.6 122.3 %while.56 = (s32[]{:T(128)}, f32[4,4,128]{2,1,0:T(4,128)S(1)}, f32[4,4,128]{2,1,0:T(4,128)S(1)}, f32[4,4,128,128]{3,2,1,0:T(8,128)}, s32[8]{0:T(128)S(1)}, /*ind...) while((s32[]{:T(128)}, f32[4,4,128]{2,1,0:T(4,128)S(1)}, ...), condition=%wide.region_4.5_spmd.clone.clone, body=%wide.region_1.0_spmd.clone.sunk.clone | while | flops 551365248 | bytes 35525820 | solution.py:122
  503.9 2.8 fusion.97
  506.7 3.3 fusion.98
  517.9 2.8 fusion.97
  520.8 3.3 fusion.98
  524.2 3.7 fusion.100
  533.2 2.8 fusion.97
  536.0 3.4 fusion.98
  539.5 3.7 fusion.100
  551.4 3.3 fusion.98
  554.9 3.7 fusion.100
  566.7 3.3 fusion.98
  570.2 3.8 fusion.100
  582.2 3.4 fusion.98
  585.7 3.7 fusion.100
  597.5 3.4 fusion.98
  601.1 3.7 fusion.100
  612.8 4.0 fusion.98
  617.2 3.7 fusion.100
  623.5 95.9 %all-gather.10.cloned.1.call-done = bf16[2,2560,2048]{2,1,0:T(8,128)(2,1)} async-done(((bf16[2,80,2048]{2,1,0:T(8,128)(2,1)}), bf16[2,2560,2048]{2,1,0:T(8,128)(2,1)}) %all-gather.10.cloned.1.call-update) | async-done | bytes 20971536 | tf_op jit(solution)/shard_map/all_gather | solution.py:204
  719.4 12.7 %fusion.66 = f32[2,2560,224]{1,2,0:T(8,128)} fusion(bf16[2,2560,2048]{2,1,0:T(8,128)(2,1)} %all-gather.10.cloned.1.call-done, bf16[2,2048,224]{1,2,0:T(8,128)(2,1)S(1)} %copy-done), kind=kOutput, calls=%fused_computation.119 | convolution fusion | flops 4697620480 | bytes 27394048 | tf_op jit(solution)/shard_map/lrd,ldf->lrf/dot_general | solution.py:205
  732.1 12.3 %multiply_reduce_fusion.2 = f32[2,2560]{1,0:T(2,128)S(1)} fusion(f32[2,224]{1,0:T(2,128)S(1)} %copy-done.22, bf16[2,2560,2048]{2,1,0:T(8,128)(2,1)} %all-gather.10.cloned.1.call-done, bf16[2,2048,224]{1,2,0:T(8,128)(2,1)} %param.52, f32[2,2560,224]{1,2,0:T(8,128)} %fusion.66), kind=kOutput, calls=%fused_computation.40 | convolution fusion | flops 4707937280 | bytes 27416320 | tf_op jit(solution)/shard_map/lrd,ldf->lrf/dot_general | solution.py:208
  746.0 18.8 %while.55 = (s32[]{:T(128)}, f32[4,32,4096]{2,1,0:T(8,128)}, f32[4,32,16]{1,0,2:T(4,128)S(1)}, f32[4,32,4096]{2,1,0:T(8,128)}, f32[16,4096]{1,0:T(8,128)S(1)}, /*index=5*/f32[16,4096]{1,0:T(8,128)S(1)}) while((s32[]{:T(128)}, f32[4,32,4096]{2,1,0:T(8,128)}, f32[4,32,16]{1,0,2:T(4,128)S(1)}, f32[4,32,4096]{2,1,0:T(8,128)}, ...), condition=%wide.region_14.15_spmd.clone, body=%wide.region_12.14_spmd.sunk.clone | while | flops 8257538 | bytes 3680845 | solution.py:170
  764.8 194.5 %reduce-scatter.4.cloned.1.call-done = f32[80,2]{1,0:T(8,128)} async-done(((f32[2560,2]{1,0:T(8,128)}), f32[80,2]{1,0:T(8,128)}) %reduce-scatter.4.cloned.1.call-update) | async-done | bytes 656
  960.9 4.8 all-to-all-start.1
  965.8 6.5 multiply_reduce_fusion.3
  976.4 138.2 %all-reduce.2.cloned.1.call-done = bf16[65536]{0:T(1024)(128)(2,1)} async-done(((bf16[65536]{0:T(1024)(128)(2,1)}), bf16[65536]{0:T(1024)(128)(2,1)}) %all-reduce.2.cloned.1.call-update) | async-done | bytes 131088 | tf_op jit(solution)/shard_map/pmax | solution.py:230
  (737 shorter events, 536.5 us)
Async XLA Ops:
  7.2 712.3 %copy-start = (bf16[2,2048,224]{1,2,0:T(8,128)(2,1)S(1)}, bf16[2,2048,224]{1,2,0:T(8,128)(2,1)}, u32[]{:S(2)}) copy-start(bf16[2,2048,224]{1,2,0:T(8,128)(2,1)} %param.51) | copy-start | bytes 5505028
  7.2 491.4 %all-gather.12.cloned.1.call-start = ((), (), s32[]{:S(2)}) async-start(), calls=%async_computation.5 | async-start | bytes 4325376 | tf_op jit(solution)/shard_map/all_gather | solution.py:108
  9.0 489.6 %all-gather.14.cloned.1.call-start = ((), (), s32[]{:S(2)}) async-start(), calls=%async_computation.6 | async-start | bytes 4325376 | tf_op jit(solution)/shard_map/all_gather | solution.py:109
  10.8 612.4 %all-gather.16.cloned.1.call-start = ((), (), s32[]{:S(2)}) async-start(), calls=%async_computation.7 | async-start | bytes 4325376 | tf_op jit(solution)/shard_map/all_gather | solution.py:24
  12.3 16.6 %collective-permute-start = (bf16[3,4096]{1,0:T(4,128)(2,1)}, bf16[3,4096]{1,0:T(4,128)(2,1)S(1)}, u32[]{:S(2)}, u32[]{:S(2)}) collective-permute-start(bf16[3,4096]{1,0:T(4,128)(2,1)} %slice_bitcast_fusion), channel_id=1, source_target_pairs={{0,1},{1,2},{2,3},{3,4},{4,5},{5,6},{6,7},{7,8},{8,9},{9,10},{10,1... | collective-permute-start | bytes 73736 | tf_op jit(solution)/shard_map/ppermute | solution.py:18
  19.9 5.7 copy-start.7
  19.9 7.5 copy-start.14
  19.9 8.3 copy-start.9
  19.9 9.0 copy-start.4
  25.6 3.6 copy-start.8
  26.3 596.9 %all-gather.18.cloned.1.call-start = ((), (), s32[]{:S(2)}) async-start(), calls=%async_computation.8 | async-start | bytes 4325376 | tf_op jit(solution)/shard_map/all_gather | solution.py:24
  31.9 442.4 %copy-start.17 = (s32[1,128,2]{1,2,0:T(2,128)S(1)}, s32[1,128,2]{1,2,0:T(2,128)}, u32[]{:S(2)}) copy-start(s32[1,128,2]{1,2,0:T(2,128)} %param.54) | copy-start | bytes 3076
  31.9 442.7 %copy-start.23 = (s32[8]{0:T(128)S(1)}, s32[8]{0:T(128)}, u32[]{:S(2)}) copy-start(s32[8]{0:T(128)} %param.56) | copy-start | bytes 100
  474.2 4.5 copy-start.21
  474.3 245.2 %all-gather.10.cloned.1.call-start = ((), (), s32[]{:S(2)}) async-start(), calls=%async_computation.3 | async-start | bytes 21626880 | tf_op jit(solution)/shard_map/all_gather | solution.py:204
  480.3 17.0 %copy-start.10 = (f32[1,128,16]{1,2,0:T(8,128)S(1)}, f32[1,128,16]{1,2,0:T(8,128)}, u32[]{:S(2)}) copy-start(f32[1,128,16]{1,2,0:T(8,128)} %param.41) | copy-start | bytes 24580
  480.3 17.1 %copy-start.6 = (bf16[1,128,2048]{2,1,0:T(8,128)(2,1)S(1)}, bf16[1,128,2048]{2,1,0:T(8,128)(2,1)}, u32[]{:S(2)}) copy-start(bf16[1,128,2048]{2,1,0:T(8,128)(2,1)} %param.34) | copy-start | bytes 1572868
  497.1 462.2 %reduce-scatter.4.cloned.1.call-start = ((), (), s32[]{:S(2)}) async-start(), calls=%async_computation.9 | async-start | bytes 1351680
  498.6 122.3 %copy-start.13 = (f32[2048]{0:T(1024)S(1)}, f32[2048]{0:T(1024)}, u32[]{:S(2)}) copy-start(f32[2048]{0:T(1024)} %param.48) | copy-start | bytes 24580
  566.7 3.6 copy-start.2
  582.2 3.5 copy-start.2
  597.5 3.5 copy-start.2
  612.8 4.4 copy-start.2
  623.5 108.7 %copy-start.22 = (f32[2,224]{1,0:T(2,128)S(1)}, f32[2,224]{1,0:T(2,128)}, u32[]{:S(2)}) copy-start(f32[2,224]{1,0:T(2,128)} %param.53) | copy-start | bytes 5380
  746.0 219.7 %copy-start.5 = (bf16[1,128,4096]{2,1,0:T(8,128)(2,1)S(1)}, bf16[1,128,4096]{2,1,0:T(8,128)(2,1)}, u32[]{:S(2)}) copy-start(bf16[1,128,4096]{2,1,0:T(8,128)(2,1)} %param.38) | copy-start | bytes 3145732
  746.0 219.7 %copy-start.11 = (f32[4096]{0:T(1024)S(1)}, f32[4096]{0:T(1024)}, u32[]{:S(2)}) copy-start(f32[4096]{0:T(1024)} %param.47) | copy-start | bytes 49156
  960.9 11.4 %all-to-all-start.1 = ((f32[2,8,10]{2,0,1:T(2,128)}), f32[2,8,10]{2,0,1:T(2,128)S(1)}, u32[]{:S(2)}, u32[]{:S(2)}) async-start(f32[2,8,10]{2,0,1:T(2,128)} %copy.87), calls=%async_computation.1 | async-start | bytes 16384 | tf_op jit(solution)/shard_map/all_to_all | solution.py:212
  965.7 148.9 %all-reduce.2.cloned.1.call-start = ((), (), s32[]{:S(2)}) async-start(), calls=%async_computation.4 | async-start | bytes 262144 | tf_op jit(solution)/shard_map/pmax | solution.py:230
  965.7 6.5 copy-start.16
  965.7 6.7 copy-start.18
  965.8 6.7 copy-start.19
  965.8 150.1 %copy-start.1 = (bf16[2,2048,224]{1,2,0:T(8,128)(2,1)S(1)}, bf16[2,2048,224]{1,2,0:T(8,128)(2,1)}, u32[]{:S(2)}) copy-start(bf16[2,2048,224]{1,2,0:T(8,128)(2,1)} %param.51) | copy-start | bytes 5505028
  (9 other events, 27.5 us)
Sparse Core Ops, SparseCore 0:
  10.5 86.1 all-gather.11
  99.1 83.3 all-gather.13
  185.1 81.9 all-gather.15
  474.4 83.8 all-gather.17
  560.8 158.6 all-gather.9
  746.1 213.1 reduce-scatter.3
  975.4 139.1 all-reduce.1
where the time goes:
time: 1130 us; the launch traced here: 1120 us
  waiting for transfers between devices  429 us (38%)
  local copies, waits for them, and re-layouts  340 us (30%)
  other arithmetic  220 us (19%)
  matrix products  77.8 us (7%)
  loops' own time  17.7 us (2%)
  blocking collectives  15 us (1%)
  between operations  14.6 us (1%)
    dynamic_update_slice x128, local copies, waits for them, and re-layouts, shards(): lax.scan(emit_rows, zero_state, (step_size, b_rows, c_rows, conved))  207 us
    unnamed x8, waiting for transfers between devices  195 us
    pmax x1, waiting for transfers between devices, shards(): lax.pmax(pooled.astype(jnp.bfloat16), 'context').astype(pooled.dtype)  138 us
    dynamic_slice x128, other arithmetic, shards(): lax.scan(emit_rows, zero_state, (step_size, b_rows, c_rows, conved))  127 us
    all_gather x1, waiting for transfers between devices, shards(): row_piece = lax.all_gather(slot_rows, 'context', axis=1, tiled=True)  95.9 us
    mul x128, local copies, waits for them, and re-layouts, emit_rows(): (size_now * x_now)[None, :] * b_now[:, None]  89 us
    dot_general x8, matrix products, key_block(): jnp.einsum('gqtr,rgd->gqtd', exp_scores.astype(jnp.bfloat16), value_heads...  28.6 us
    reduce_sum x8, other arithmetic, key_block(): running_sum = running_sum * factor + jnp.sum(exp_scores, axis=-1)  27.5 us
  transfers between devices with their start and end apart: 9, of which 3 were waited for; matrix products, arithmetic and copies ran while one was open for 54% of the time, Pallas kernels for 0%

commit v1 on v0

--- a/solution.py
+++ b/solution.py
@@ -201,7 +201,12 @@
     ).astype(jnp.bfloat16)
     arrived = lax.all_to_all(outgoing, "expert", split_axis=1, concat_axis=1, tiled=True)
     slot_rows = arrived.reshape(local_experts, axis_experts * capacity, normed.shape[1])
-    row_piece = lax.all_gather(slot_rows, "context", axis=1, tiled=True)
+    row_piece = jnp.concatenate(
+        lax.all_to_all(
+            jnp.stack([slot_rows for _ in range(lax.psum(1, "context"))], axis=0), "context", 0, 0
+        ),
+        axis=1,
+    )
     gate_part = jnp.einsum(
         "lrd,ldf->lrf", row_piece, expert_gate, preferred_element_type=jnp.float32
     )

time: 1130 us -> 1180 us (1.044)
  waiting for transfers between devices: 429 us -> 548 us
  local copies, waits for them, and re-layouts: 340 us -> 278 us
  starting transfers between devices: 9.09 us -> 24.6 us
  blocking collectives: 15 us -> 0 us
    all_gather x2, waiting for transfers between devices: 0.01 us -> 182 us  [prefix(): lax.all_gather(a.astype(kind), axis)]
    all_gather x1 -> x0, waiting for transfers between devices: 95.9 us -> none  [shards(): row_piece = lax.all_gather(slot_rows, 'context', axis=1, tiled=True)]
    mul x128, local copies, waits for them, and re-layouts: 89 us -> 1.68 us  [emit_rows(): (size_now * x_now)[None, :] * b_now[:, None]]
    unnamed x8 -> x7, waiting for transfers between devices: 195 us -> 227 us
    all_to_all x0 -> x2, starting transfers between devices: none -> 17.1 us  [the longest x1 10.7 us: shards(): lax.all_to_all(jnp.stack([slot_rows for _ in range(lax.psum(1, 'context')...]
    reshape x1, local copies, waits for them, and re-layouts: 1.08 us -> 17.6 us  [shards(): jnp.concatenate(lax.all_to_all(jnp.stack([slot_rows for _ in range(lax.ps...]
    all_to_all x1 -> x0, blocking collectives: 15 us -> none  [shards(): lax.all_to_all(outgoing, 'expert', split_axis=1, concat_axis=1, tiled=True)]
  transfers between devices with their start and end apart: 9 -> 10, of which waited for: 3 -> 4; matrix products, arithmetic and copies ran while one was open for 54% -> 44% of each run, Pallas kernels for 0% -> 0%
where the time goes in v1:
time: 1180 us
  waiting for transfers between devices  548 us (46%)
  local copies, waits for them, and re-layouts  278 us (24%)
  other arithmetic  217 us (18%)
  matrix products  76.3 us (6%)
  starting transfers between devices  24.6 us (2%)
  loops' own time  18.4 us (2%)
  between operations  14.6 us (1%)
    unnamed x7, waiting for transfers between devices  227 us
    dynamic_update_slice x128, local copies, waits for them, and re-layouts, shards(): lax.scan(emit_rows, zero_state, (step_size, b_rows, c_rows, conved))  207 us
    all_gather x2, waiting for transfers between devices, prefix(): lax.all_gather(a.astype(kind), axis)  182 us
    pmax x1, waiting for transfers between devices, shards(): lax.pmax(pooled.astype(jnp.bfloat16), 'context').astype(pooled.dtype)  138 us
    dynamic_slice x128, other arithmetic, shards(): lax.scan(emit_rows, zero_state, (step_size, b_rows, c_rows, conved))  127 us
    dot_general x8, matrix products, key_block(): jnp.einsum('gqtr,rgd->gqtd', exp_scores.astype(jnp.bfloat16), value_heads...  28.4 us
    reduce_sum x8, other arithmetic, key_block(): running_sum = running_sum * factor + jnp.sum(exp_scores, axis=-1)  26.7 us
  transfers between devices with their start and end apart: 10, of which 4 were waited for; matrix products, arithmetic and copies ran while one was open for 44% of the time, Pallas kernels for 0%

profile of v1, /device:TPU:2, one launch (start us, length us, event | category | flops | bytes accessed | tf_op | source)
XLA Modules:
  0.0 1177.4 jit_solution(16427792794597735197)
XLA Ops:
  17.1 6.4 all-to-all-start
  29.3 4.7 reduce_window_sum.22
  45.4 7.4 stack.3
  52.8 10.7 all-to-all-start.1
  63.6 355.8 %while.57 = (s32[]{:T(128)}, f32[16,4096]{1,0:T(8,128)S(1)}, f32[128,4096]{1,0:T(8,128)}, f32[128,4096]{1,0:T(8,128)}, f32[16,4096]{1,0:T(8,128)S(1)}, /*index=5...) while((s32[]{:T(128)}, f32[16,4096]{1,0:T(8,128)S(1)}, ...), condition=%wide.region_8.9_spmd.clone.clone, body=%wide.region_6.8_spmd.clone.sunk.clone | while | flops 458755 | bytes 934379 | solution.py:153
  420.3 119.1 %while.56 = (s32[]{:T(128)}, f32[4,4,128]{2,1,0:T(4,128)S(1)}, f32[4,4,128]{2,1,0:T(4,128)S(1)}, f32[4,4,128,128]{3,2,1,0:T(8,128)}, s32[8]{0:T(128)S(1)}, /*ind...) while((s32[]{:T(128)}, f32[4,4,128]{2,1,0:T(4,128)S(1)}, ...), condition=%wide.region_4.5_spmd.clone.clone, body=%wide.region_1.0_spmd.clone.sunk.clone | while | flops 551365248 | bytes 35525820 | solution.py:122
  428.3 3.3 fusion.98
  442.1 3.3 fusion.98
  445.5 3.7 fusion.100
  457.1 3.3 fusion.98
  460.6 3.7 fusion.100
  472.2 3.3 fusion.98
  475.6 3.7 fusion.100
  484.4 2.8 fusion.97
  487.2 3.3 fusion.98
  490.7 3.7 fusion.100
  502.3 3.3 fusion.98
  505.7 3.7 fusion.100
  517.3 3.4 fusion.98
  520.8 3.7 fusion.100
  532.3 3.3 fusion.98
  535.8 3.7 fusion.100
  541.1 100.9 %all-gather.13.cloned.1.call-done = bf16[512,4096]{1,0:T(8,128)(2,1)} async-done(((bf16[16,4096]{1,0:T(8,128)(2,1)}), bf16[512,4096]{1,0:T(8,128)(2,1)}) %all-gather.13.cloned.1.call-update) | async-done | bytes 4194320 | tf_op jit(solution)/shard_map/all_gather | solution.py:24
  642.0 81.5 %all-gather.15.cloned.1.call-done = bf16[512,4096]{1,0:T(8,128)(2,1)} async-done(((bf16[16,4096]{1,0:T(8,128)(2,1)}), bf16[512,4096]{1,0:T(8,128)(2,1)}) %all-gather.15.cloned.1.call-update) | async-done | bytes 4194320 | tf_op jit(solution)/shard_map/all_gather | solution.py:24
  723.6 17.6 %copy.88 = bf16[2,32,80,2048]{3,2,1,0:T(8,128)(2,1)} copy(bf16[2,32,80,2048]{3,2,0,1:T(8,128)(2,1)} %bitcast.34) | data formatting | bytes 41943040 | tf_op jit(solution)/shard_map/reshape | solution.py:204
  741.2 12.6 %fusion.66 = f32[2,2560,224]{1,2,0:T(8,128)} fusion(bf16[2,2560,2048]{2,1,0:T(8,128)(2,1)} %bitcast.185, bf16[2,2048,224]{1,2,0:T(8,128)(2,1)S(1)} %copy-done), kind=kOutput, calls=%fused_computation.119 | convolution fusion | flops 4697620480 | bytes 27394048 | tf_op jit(solution)/shard_map/lrd,ldf->lrf/dot_general | solution.py:210
  753.9 12.3 %multiply_reduce_fusion.2 = f32[2,2560]{1,0:T(2,128)S(1)} fusion(f32[2,224]{1,0:T(2,128)S(1)} %copy-done.20, bf16[2,2560,2048]{2,1,0:T(8,128)(2,1)} %bitcast.186, bf16[2,2048,224]{1,2,0:T(8,128)(2,1)} %param.52, f32[2,2560,224]{1,2,0:T(8,128)} %fusion.66), kind=kOutput, calls=%fused_computation.40 | convolution fusion | flops 4707937280 | bytes 27416320 | tf_op jit(solution)/shard_map/lrd,ldf->lrf/dot_general | solution.py:213
  767.8 18.8 %while.55 = (s32[]{:T(128)}, f32[4,32,4096]{2,1,0:T(8,128)}, f32[4,32,16]{1,0,2:T(4,128)S(1)}, f32[4,32,4096]{2,1,0:T(8,128)}, f32[16,4096]{1,0:T(8,128)S(1)}, /*index=5*/f32[16,4096]{1,0:T(8,128)S(1)}) while((s32[]{:T(128)}, f32[4,32,4096]{2,1,0:T(8,128)}, f32[4,32,16]{1,0,2:T(4,128)S(1)}, f32[4,32,4096]{2,1,0:T(8,128)}, ...), condition=%wide.region_14.15_spmd.clone, body=%wide.region_12.14_spmd.sunk.clone | while | flops 8257538 | bytes 3680845 | solution.py:170
  786.6 227.3 %reduce-scatter.4.cloned.1.call-done = f32[80,2]{1,0:T(8,128)} async-done(((f32[2560,2]{1,0:T(8,128)}), f32[80,2]{1,0:T(8,128)}) %reduce-scatter.4.cloned.1.call-update) | async-done | bytes 656
  1015.4 4.9 all-to-all-start.2
  1020.3 6.8 multiply_reduce_fusion.3
  1031.3 138.0 %all-reduce.2.cloned.1.call-done = bf16[65536]{0:T(1024)(128)(2,1)} async-done(((bf16[65536]{0:T(1024)(128)(2,1)}), bf16[65536]{0:T(1024)(128)(2,1)}) %all-reduce.2.cloned.1.call-update) | async-done | bytes 131088 | tf_op jit(solution)/shard_map/pmax | solution.py:235
  (733 shorter events, 458.0 us)
Async XLA Ops:
  7.2 734.1 %copy-start = (bf16[2,2048,224]{1,2,0:T(8,128)(2,1)S(1)}, bf16[2,2048,224]{1,2,0:T(8,128)(2,1)}, u32[]{:S(2)}) copy-start(bf16[2,2048,224]{1,2,0:T(8,128)(2,1)} %param.51) | copy-start | bytes 5505028
  7.2 7.6 copy-start.5
  7.2 7.6 copy-start.14
  7.2 413.1 %all-gather.9.cloned.1.call-start = ((), (), s32[]{:S(2)}) async-start(), calls=%async_computation.5 | async-start | bytes 4325376 | tf_op jit(solution)/shard_map/all_gather | solution.py:108
  9.1 411.2 %all-gather.11.cloned.1.call-start = ((), (), s32[]{:S(2)}) async-start(), calls=%async_computation.6 | async-start | bytes 4325376 | tf_op jit(solution)/shard_map/all_gather | solution.py:109
  10.8 4.3 copy-start.19
  15.6 11.1 copy-start.4
  15.6 11.1 copy-start.11
  17.1 27.0 %all-to-all-start = ((bf16[2,8,10,2048]{3,0,2,1:T(2,128)(2,1)}), bf16[2,8,10,2048]{3,0,2,1:T(2,128)(2,1)}, u32[]{:S(2)}, u32[]{:S(2)}) async-start(bf16[2,8,10,2048]{3,0,2,1:T(2,128)(2,1)} %copy.86), calls=%async_computation | async-start | bytes 1310720 | tf_op jit(solution)/shard_map/all_to_all | solution.py:202
  23.5 618.5 %all-gather.13.cloned.1.call-start = ((), (), s32[]{:S(2)}) async-start(), calls=%async_computation.7 | async-start | bytes 4325376 | tf_op jit(solution)/shard_map/all_gather | solution.py:24
  24.4 14.2 %collective-permute-start = (bf16[3,4096]{1,0:T(4,128)(2,1)S(1)}, bf16[3,4096]{1,0:T(4,128)(2,1)S(1)}, u32[]{:S(2)}, u32[]{:S(2)}) collective-permute-start(bf16[3,4096]{1,0:T(4,128)(2,1)S(1)} %slice_bitcast_fusion), channel_id=1, source_target_pairs={{0,1},{1,2},{2,3},{3,4},{4,5},{5,6},{6,7},{7,8},{8,9},{9,10},{10,1... | collective-permute-start | bytes 73736 | tf_op jit(solution)/shard_map/ppermute | solution.py:18
  29.2 5.7 copy-start.7
  29.2 6.4 copy-start.17
  29.2 6.5 copy-start.18
  29.2 6.5 copy-start.9
  29.2 6.5 copy-start.21
  29.3 6.6 copy-start.10
  29.3 6.8 copy-start.16
  29.3 6.9 copy-start.6
  37.2 4.3 copy-start.8
  52.8 670.8 %all-to-all-start.1 = ((bf16[32,2,80,2048]{3,2,1,0:T(8,128)(2,1)}), bf16[32,2,80,2048]{3,2,1,0:T(8,128)(2,1)}, u32[]{:S(2)}, u32[]{:S(2)}) async-start(bf16[32,2,80,2048]{3,2,1,0:T(8,128)(2,1)} %stack.3), calls=%async_computation.1 | async-start | bytes 41943040 | tf_op jit(solution)/shard_map/all_to_all | solution.py:205
  63.5 660.0 %all-gather.15.cloned.1.call-start = ((), (), s32[]{:S(2)}) async-start(), calls=%async_computation.8 | async-start | bytes 4325376 | tf_op jit(solution)/shard_map/all_gather | solution.py:24
  420.0 593.8 %reduce-scatter.4.cloned.1.call-start = ((), (), s32[]{:S(2)}) async-start(), calls=%async_computation.9 | async-start | bytes 1351680
  420.3 119.2 %copy-start.15 = (f32[2048]{0:T(1024)S(1)}, f32[2048]{0:T(1024)}, u32[]{:S(2)}) copy-start(f32[2048]{0:T(1024)} %param.48) | copy-start | bytes 24580
  517.3 3.5 copy-start.2
  532.3 3.5 copy-start.2
  741.2 12.6 %copy-start.20 = (f32[2,224]{1,0:T(2,128)S(1)}, f32[2,224]{1,0:T(2,128)}, u32[]{:S(2)}) copy-start(f32[2,224]{1,0:T(2,128)} %param.53) | copy-start | bytes 5380
  767.7 252.5 %copy-start.12 = (f32[4096]{0:T(1024)S(1)}, f32[4096]{0:T(1024)}, u32[]{:S(2)}) copy-start(f32[4096]{0:T(1024)} %param.47) | copy-start | bytes 49156
  767.8 252.5 %copy-start.13 = (f32[4096]{0:T(1024)S(1)}, f32[4096]{0:T(1024)}, u32[]{:S(2)}) copy-start(f32[4096]{0:T(1024)} %param.46) | copy-start | bytes 49156
  1015.4 11.7 all-to-all-start.2
  1020.3 149.0 %all-reduce.2.cloned.1.call-start = ((), (), s32[]{:S(2)}) async-start(), calls=%async_computation.4 | async-start | bytes 262144 | tf_op jit(solution)/shard_map/pmax | solution.py:235
  1020.3 150.3 %copy-start.1 = (bf16[2,2048,224]{1,2,0:T(8,128)(2,1)S(1)}, bf16[2,2048,224]{1,2,0:T(8,128)(2,1)}, u32[]{:S(2)}) copy-start(bf16[2,2048,224]{1,2,0:T(8,128)(2,1)} %param.51) | copy-start | bytes 5505028
  (7 other events, 22.1 us)
Sparse Core Ops, SparseCore 0:
  10.5 159.2 all-gather.8
  172.3 247.4 all-gather.10
  422.4 219.5 all-gather.12
  644.5 79.0 all-gather.14
  767.9 245.9 reduce-scatter.3
  1030.2 139.0 all-reduce.1
